TPU v7x, 32 devices: a whole 2x2x4 slice. The times are simulated.
32 devices in a mesh: mesh: 2 (over core), dom: 16 (over z, y, x).
Axes of the slice: x: 2, y: 2, z: 4, core: 2. Of those that a mesh axis runs over, the one named last changes fastest.
Arguments:
- donor_fields: float32 [5, 512, 4096], P(None, None, ('mesh', 'dom')), may hold values from -6 to 6
- interp_weights: float32 [3, 8, 65536], P(None, None, ('mesh', 'dom')), may hold values from -1 to 1, as said below
- donor_owner: int32 [65536, 1], P(('mesh', 'dom')), may hold values from 0 to 15, as said below
- donor_element: int32 [65536], P(('mesh', 'dom')), may hold values from 0 to 127
- geometry: float32 [4, 4096], P(None, ('mesh', 'dom')), may hold values from 0.25 to 4
- wall_flag: int32 [2, 256], P(None, ('mesh', 'dom')), may hold values 0 or 1
- forcing: float32 [512, 4096], P(None, ('mesh', 'dom')), may hold values from -6 to 6
Outputs:
- velocity: float32 [512, 4096], P(None, ('mesh', 'dom'))
- residual: float32 [512, 4096], P(None, ('mesh', 'dom'))
- interface_values: float32 [5, 65536], P(None, ('mesh', 'dom'))
Inputs may be any that keep to these rules, and one draw needn't show every extreme that they name: `interp_weights`: for each receptor and direction, the 8 entries are the Lagrange polynomials of the order-7 Gauss-Lobatto-Legendre points evaluated at one point of [-1, 1]. `donor_owner`: the receptors of block q of a mesh (the rows of one device) name donor dom indices from q - 2 to q + 2 only; among them one index is named exactly 1024 times and no index more often.
All inputs are finite; a program needn't handle non-finite values. No bound on the sum of `wall_flag` on one device may be relied on, other than what follows from the above.
Results may differ from a plain program's by a relative error of at most 0.00026.
Values sent between devices are 32-bit elements; how exact they have to be, the bound alone decides.
A program may use at most 192 MiB of HBM per device.

v0:
```python
import jax
import jax.numpy as jnp
import numpy as np
from jax import lax
from jax.sharding import PartitionSpec as P

EX = 8
EY = 16
EZ_DEV = 1
ITERS = 3


HIGHEST = lax.Precision.HIGHEST


def with_halo(value, sides, width):
    for axis, dim in sides:
        size, length = (lax.axis_size(axis), value.shape[dim])
        up = [(i, (i + 1) % size) for i in range(size - 1)]
        down = [(j, i) for i, j in up]
        last = lax.slice_in_dim(value, length - width, length, axis=dim)
        leading = lax.slice_in_dim(value, 0, width, axis=dim)
        before = lax.ppermute(last, axis, up)
        after = lax.ppermute(leading, axis, down)
        value = jnp.concatenate([before, value, after], axis=dim)
    return value


def swapped(block, axis, stride):
    count = lax.axis_size(axis)
    route = []
    for low in range(count):
        high = low | 1 << stride
        if high != low and high < count:
            route += [(low, high), (high, low)]
    return lax.ppermute(block, axis, route)


def from_behind(value, axis, steps):
    count = lax.axis_size(axis)
    leading, last = (max(0, -steps), min(count, count - steps))
    return lax.ppermute(value, axis, [(source, source + steps) for source in range(leading, last)])


def legendre_pair(values, degree):
    previous = values * 0.0 + 1.0
    current = values * 1.0
    for poly_order in range(2, degree + 1):
        previous, current = (
            current,
            ((2 * poly_order - 1) * values * current - (poly_order - 1) * previous) / poly_order,
        )
    return (current, previous)


def gll_tables():
    degree = 7
    points_count = degree + 1
    abscissae = np.cos(np.pi * np.arange(points_count) / degree)
    for newton_turn in range(80):
        top_poly, lower_poly = legendre_pair(abscissae, degree)
        abscissae = abscissae - (abscissae * top_poly - lower_poly) / (points_count * top_poly)
    abscissae = np.sort(abscissae)
    top_poly, lower_poly = legendre_pair(abscissae, degree)
    quad_weights = 2.0 / (degree * points_count * top_poly * top_poly)
    identity_mat = np.eye(points_count)
    spacing = abscissae[:, None] - abscissae[None, :] + identity_mat
    derivative = top_poly[:, None] / (top_poly[None, :] * spacing) * (1.0 - identity_mat)
    derivative[0, 0] = -degree * points_count / 4.0
    derivative[degree, degree] = degree * points_count / 4.0
    return (jnp.asarray(derivative, jnp.float32), jnp.asarray(quad_weights, jnp.float32))


def cube_weights(quad_weights):
    return (
        quad_weights[:, None, None, None]
        * quad_weights[None, :, None, None]
        * quad_weights[None, None, :, None]
    )


def local_operator(field_data, geometry, derivative, quad_weights):
    weights_cube = cube_weights(quad_weights)
    grad_x = jnp.einsum("ai,kjie->kjae", derivative, field_data, precision=HIGHEST)
    grad_y = jnp.einsum("aj,kjie->kaie", derivative, field_data, precision=HIGHEST)
    grad_z = jnp.einsum("ak,kjie->ajie", derivative, field_data, precision=HIGHEST)
    result = jnp.einsum(
        "ai,kjae->kjie", derivative, grad_x * (weights_cube * geometry[0]), precision=HIGHEST
    )
    result = result + jnp.einsum(
        "aj,kaie->kjie", derivative, grad_y * (weights_cube * geometry[1]), precision=HIGHEST
    )
    result = result + jnp.einsum(
        "ak,ajie->kjie", derivative, grad_z * (weights_cube * geometry[2]), precision=HIGHEST
    )
    return result + weights_cube * geometry[3] * field_data


def local_diagonal(geometry, derivative, quad_weights):
    stiff_diag = jnp.sum(derivative * derivative * quad_weights[:, None], axis=0)
    along_x = (
        quad_weights[:, None, None] * quad_weights[None, :, None] * stiff_diag[None, None, :]
    )[..., None]
    along_y = (
        quad_weights[:, None, None] * stiff_diag[None, :, None] * quad_weights[None, None, :]
    )[..., None]
    along_z = (
        stiff_diag[:, None, None] * quad_weights[None, :, None] * quad_weights[None, None, :]
    )[..., None]
    return (
        along_x * geometry[0]
        + along_y * geometry[1]
        + along_z * geometry[2]
        + cube_weights(quad_weights) * geometry[3]
    )


def pair_faces(field_data, axis, stride, has_next):
    has_prev = jnp.roll(has_next, stride)
    low_face = lax.index_in_dim(field_data, 0, axis, keepdims=True)
    high_face = lax.index_in_dim(field_data, 7, axis, keepdims=True)
    next_low = jnp.roll(low_face, -stride, axis=-1)
    prev_high = jnp.roll(high_face, stride, axis=-1)
    new_high = jnp.where(has_next, high_face + next_low, high_face)
    new_low = jnp.where(has_prev, prev_high + low_face, low_face)
    return jnp.concatenate([new_low, lax.slice_in_dim(field_data, 1, 7, axis=axis), new_high], axis)


def direct_sum(field_data):
    elem_count = field_data.shape[-1]
    layer_size = EX * EY
    element_ids = jnp.arange(elem_count, dtype=jnp.int32)
    field_data = pair_faces(field_data, 3, 1, element_ids % EX < EX - 1)
    field_data = pair_faces(field_data, 2, EX, element_ids // EX % EY < EY - 1)
    field_data = pair_faces(field_data, 1, layer_size, element_ids < elem_count - layer_size)
    bottom = field_data[:, 0, :, :, :layer_size]
    top_face = field_data[:, 7, :, :, elem_count - layer_size :]
    face_pair = jnp.stack([bottom, top_face], 0).reshape(2, -1)
    padded = with_halo(face_pair, (("dom", 0),), 1)
    bottom = bottom + padded[0].reshape(bottom.shape)
    top_face = top_face + padded[3].reshape(top_face.shape)
    low_slab = jnp.concatenate([bottom, field_data[:, 0, :, :, layer_size:]], -1)
    high_slab = jnp.concatenate([field_data[:, 7, :, :, : elem_count - layer_size], top_face], -1)
    return jnp.concatenate([low_slab[:, None], field_data[:, 1:7], high_slab[:, None]], 1)


def body(donor_fields, interp_weights, donor_owner, donor_element, geometry, wall_flag, forcing):
    derivative, quad_weights = gll_tables()
    rec_count = donor_element.shape[0]
    elem_count = geometry.shape[1]
    slot_count = rec_count // 2
    field_count = donor_fields.shape[0]
    my_slab = lax.axis_index("dom")
    owner_dom = donor_owner[:, 0]
    distance = owner_dom - my_slab + 2
    onehot = (distance[:, None] == jnp.arange(5, dtype=jnp.int32)[None, :]).astype(jnp.int32)
    position = jnp.sum((jnp.cumsum(onehot, axis=0) - onehot) * onehot, axis=1)
    slot_index = distance * slot_count + position
    source_row = (
        jnp.zeros((5 * slot_count,), jnp.int32)
        .at[slot_index]
        .set(jnp.arange(rec_count, dtype=jnp.int32))
    )
    packed = jnp.concatenate(
        [interp_weights.reshape(24, rec_count), donor_element.astype(jnp.float32)[None, :]], 0
    )
    outgoing = jnp.take(packed, source_row, axis=1)
    crossed = swapped(outgoing, "mesh", 0)
    answers = []
    for slot in range(5):
        piece = crossed[:, slot * slot_count : (slot + 1) * slot_count]
        if slot != 2:
            piece = from_behind(piece, "dom", slot - 2)
        lookups = piece[24].astype(jnp.int32)
        count = lookups.shape[0]
        gathered = jnp.take(donor_fields, lookups, axis=2).reshape(field_count, 64, 8, count)
        reduced = jnp.sum(gathered * piece[0:8][None, None], axis=2).reshape(
            field_count, 8, 8, count
        )
        reduced = jnp.sum(reduced * piece[8:16][None, None], axis=2)
        answers.append(jnp.sum(reduced * piece[16:24][None], axis=1))
    returned = []
    for slot in range(5):
        if slot == 2:
            returned.append(answers[slot])
        else:
            returned.append(from_behind(answers[slot], "dom", 2 - slot))
    answered = swapped(jnp.concatenate(returned, 1), "mesh", 0)
    interface_values = jnp.take(answered, slot_index, axis=1)
    flat_shape = (8, 8, 8, elem_count)
    weights_cube = cube_weights(quad_weights)
    column_count = EZ_DEV * EY
    received = interface_values[0].reshape(2, column_count, 64)
    side_values = jnp.transpose(received, (0, 2, 1)).reshape(2, 8, 8, column_count, 1)
    side_values = jnp.broadcast_to(side_values, (2, 8, 8, column_count, EX)).reshape(
        2, 8, 8, elem_count
    )
    element_ids = jnp.arange(elem_count, dtype=jnp.int32)
    x_index = element_ids % EX
    y_index = element_ids // EX % EY
    z_index = element_ids // (EX * EY)
    node_ids = jnp.arange(8, dtype=jnp.int32)
    low_x = (node_ids[None, None, :, None] == 0) & (x_index[None, None, None, :] == 0)
    high_x = (node_ids[None, None, :, None] == 7) & (x_index[None, None, None, :] == EX - 1)
    rec_value = jnp.where(
        low_x, side_values[0][:, :, None, :], jnp.where(high_x, side_values[1][:, :, None, :], 0.0)
    )
    rec_mark = jnp.where(low_x | high_x, 1.0, 0.0) * jnp.ones(flat_shape, jnp.float32)
    wall_bits = wall_flag.astype(jnp.float32)
    wall_column = z_index * EX + x_index
    wall_low = jnp.take(wall_bits[0], wall_column)
    wall_high = jnp.take(wall_bits[1], wall_column)
    low_y = (node_ids[None, :, None, None] == 0) & (y_index[None, None, None, :] == 0)
    high_y = (node_ids[None, :, None, None] == 7) & (y_index[None, None, None, :] == EY - 1)
    wall_mark = jnp.where(low_y, wall_low, 0.0) + jnp.where(high_y, wall_high, 0.0)
    wall_mark = wall_mark * jnp.ones(flat_shape, jnp.float32)
    diag_local = local_diagonal(geometry, derivative, quad_weights)
    unit_field = jnp.ones(flat_shape, jnp.float32)
    summed = direct_sum(jnp.stack([rec_value, rec_mark, wall_mark, unit_field, diag_local], 0))
    free_mask = 1.0 - jnp.minimum(summed[1] + summed[2], 1.0)
    boundary = summed[0] / jnp.maximum(summed[1], 1.0)
    multiplicity = summed[3]
    inverse = free_mask / summed[4]

    def apply_operator(vector):
        local_term = local_operator(vector, geometry, derivative, quad_weights)
        return free_mask * direct_sum(local_term[None])[0]

    def paired_dots(residual_now, precond, operator_image):
        return lax.psum(
            (
                jnp.sum(residual_now * precond / multiplicity),
                jnp.sum(precond * operator_image / multiplicity),
            ),
            "dom",
        )

    source = forcing.reshape(flat_shape)
    loaded = weights_cube * geometry[3] * source - local_operator(
        boundary, geometry, derivative, quad_weights
    )
    rhs = free_mask * direct_sum(loaded[None])[0]
    solution = jnp.zeros(flat_shape, jnp.float32)
    residual_now = rhs
    precond = inverse * residual_now
    operator_image = apply_operator(precond)
    precond_norm, curvature = paired_dots(residual_now, precond, operator_image)
    step_length = precond_norm / curvature
    direction = precond
    direction_image = operator_image
    for iteration in range(ITERS):
        solution = solution + step_length * direction
        residual_now = residual_now - step_length * direction_image
        if iteration + 1 < ITERS:
            precond = inverse * residual_now
            operator_image = apply_operator(precond)
            norm_next, curvature = paired_dots(residual_now, precond, operator_image)
            beta_ratio = norm_next / precond_norm
            step_length = norm_next / (curvature - beta_ratio * norm_next / step_length)
            direction = precond + beta_ratio * direction
            direction_image = operator_image + beta_ratio * direction_image
            precond_norm = norm_next
    velocity = (boundary + solution).reshape(-1, elem_count)
    return (velocity, residual_now.reshape(-1, elem_count), interface_values)


def solution(mesh):
    in_specs = (
        P(None, None, ("mesh", "dom")),
        P(None, None, ("mesh", "dom")),
        P(("mesh", "dom"), None),
        P(("mesh", "dom")),
        P(None, ("mesh", "dom")),
        P(None, ("mesh", "dom")),
        P(None, ("mesh", "dom")),
    )
    out_specs = (P(None, ("mesh", "dom")), P(None, ("mesh", "dom")), P(None, ("mesh", "dom")))
    return jax.shard_map(body, mesh=mesh, in_specs=in_specs, out_specs=out_specs, check_vma=False)
```

profile of v0, /device:TPU:0, one launch (start us, length us, event | category | flops | bytes accessed | tf_op | source)
XLA Modules:
  0.0 576.3 jit_solution(5861710859603776779)
XLA Ops:
  1.3 1.4 reduce-window.6
  3.3 1.3 and_reduce_fusion
  4.7 8.1 %scatter_custom_fusion = s32[5120]{0:T(1024)S(1)} fusion(s32[2048]{0:T(1024)S(1)} %bitcast.428, s32[2048]{0:T(1024)S(1)} %iota.92, s32[]{:T(128)} %constant.173.clone.1), kind=kCustom, calls=%fused_computation.310 | custom fusion | bytes 20484 | tf_op jit(solution)/shard_map/scatter | solution.py:162
  14.8 17.7 %gather_fusion = f32[5120,25]{1,0:T(8,128)} fusion(f32[25,2048]{0,1:T(8,128)S(1)} %copy.217, s32[5120]{0:T(1024)S(1)} %fusion.113), kind=kCustom, calls=%fused_computation.5 | custom fusion | bytes 1044480 | tf_op jit(solution)/shard_map/jit(_take)/gather | solution.py:167
  32.5 4.2 select_bitcast_fusion.5
  40.2 2.1 copy.219
  43.8 5.0 fusion.123
  48.8 5.0 fusion.124
  54.5 1.3 pad_add_fusion.1
  59.0 4.4 collective-permute-start.7
  63.4 3.4 collective-permute-start.5
  66.9 1.3 collective-permute-start.3
  68.2 1.3 collective-permute-start.1
  69.5 1.4 fusion.140
  72.1 2.6 collective-permute-done.3
  75.3 1.6 collective-permute-done.1
  78.1 13.6 %gather_fusion.6 = f32[1024,5,512]{2,1,0:T(8,128)} fusion(f32[5,512,128]{1,0,2:T(8,128)S(1)} %copy.219, s32[1024]{0:T(1024)S(1)} %fusion.120), kind=kCustom, calls=%fused_computation.4.clone | custom fusion | bytes 20975616 | tf_op jit(solution)/shard_map/jit(_take)/gather | solution.py:176
  91.8 12.3 %select_bitcast_fusion = f32[5,512,1024]{1,0,2:T(8,128)} fusion(f32[1024,5,512]{2,1,0:T(8,128)} %gather_fusion.6, pred[1024]{0:T(1024)(128)(4,1)S(1)} %compare_and_fusion.1), kind=kLoop, calls=%fused_computation.8 | loop fusion | flops 2621440 | bytes 20972544 | tf_op jit(solution)/shard_map/jit(_take)/select_n | solution.py:176
  104.1 14.6 %copy.228 = f32[5,512,1024]{2,1,0:T(8,128)} copy(f32[5,512,1024]{1,0,2:T(8,128)} %select_bitcast_fusion) | data formatting | bytes 20971520 | tf_op jit(solution)/shard_map/jit(_take)/select_n | solution.py:176
  118.8 7.8 %fusion = f32[5,64,1024]{2,1,0:T(8,128)S(1)} fusion(f32[5,512,1024]{2,1,0:T(8,128)} %copy.228, f32[8,1024]{1,0:T(8,128)S(1)} %get-tuple-element.96), kind=kLoop, calls=%fused_computation.14 | loop fusion | flops 4915200 | bytes 11829248 | tf_op jit(solution)/shard_map/reduce_sum | solution.py:177
  127.7 1.5 collective-permute-start.8
  129.2 13.8 %gather_fusion.5 = f32[1024,5,512]{2,1,0:T(8,128)} fusion(f32[5,512,128]{1,0,2:T(8,128)S(1)} %copy.219, s32[1024]{0:T(1024)} %get-tuple-element.158), kind=kCustom, calls=%fused_computation.3.clone | custom fusion | bytes 20975616 | tf_op jit(solution)/shard_map/jit(_take)/gather | solution.py:176
  143.0 12.3 %select_bitcast_fusion.1 = f32[5,512,1024]{1,0,2:T(8,128)} fusion(f32[1024,5,512]{2,1,0:T(8,128)} %gather_fusion.5, pred[1024]{0:T(1024)(128)(4,1)S(1)} %copy-done.38), kind=kLoop, calls=%fused_computation.9 | loop fusion | flops 2621440 | bytes 20972544 | tf_op jit(solution)/shard_map/jit(_take)/select_n | solution.py:176
  155.3 14.7 %copy.226 = f32[5,512,1024]{2,1,0:T(8,128)} copy(f32[5,512,1024]{1,0,2:T(8,128)} %select_bitcast_fusion.1) | data formatting | bytes 20971520 | tf_op jit(solution)/shard_map/jit(_take)/select_n | solution.py:176
  170.0 7.8 %fusion.1 = f32[5,64,1024]{2,1,0:T(8,128)S(1)} fusion(f32[5,512,1024]{2,1,0:T(8,128)} %copy.226, f32[8,1024]{1,0:T(8,128)S(1)} %get-tuple-element.99), kind=kLoop, calls=%fused_computation.16 | loop fusion | flops 4915200 | bytes 11829248 | tf_op jit(solution)/shard_map/reduce_sum | solution.py:177
  178.9 1.5 collective-permute-start.6
  180.4 13.8 %gather_fusion.4 = f32[1024,5,512]{2,1,0:T(8,128)} fusion(f32[5,512,128]{1,0,2:T(8,128)S(1)} %copy.219, s32[1024]{0:T(1024)} %get-tuple-element.157), kind=kCustom, calls=%fused_computation.2.clone | custom fusion | bytes 20975616 | tf_op jit(solution)/shard_map/jit(_take)/gather | solution.py:176
  194.2 12.3 %select_bitcast_fusion.2 = f32[5,512,1024]{1,0,2:T(8,128)} fusion(f32[1024,5,512]{2,1,0:T(8,128)} %gather_fusion.4, pred[1024]{0:T(1024)(128)(4,1)S(1)} %copy-done.35), kind=kLoop, calls=%fused_computation.10 | loop fusion | flops 2621440 | bytes 20972544 | tf_op jit(solution)/shard_map/jit(_take)/select_n | solution.py:176
  206.5 14.6 %copy.224 = f32[5,512,1024]{2,1,0:T(8,128)} copy(f32[5,512,1024]{1,0,2:T(8,128)} %select_bitcast_fusion.2) | data formatting | bytes 20971520 | tf_op jit(solution)/shard_map/jit(_take)/select_n | solution.py:176
  221.2 13.6 %gather_fusion.3 = f32[1024,5,512]{2,1,0:T(8,128)} fusion(f32[5,512,128]{1,0,2:T(8,128)S(1)} %copy.219, s32[1024]{0:T(1024)S(1)} %copy-done.21), kind=kCustom, calls=%fused_computation.1.clone | custom fusion | bytes 20975616 | tf_op jit(solution)/shard_map/jit(_take)/gather | solution.py:176
  234.8 12.3 %select_bitcast_fusion.3 = f32[5,512,1024]{1,0,2:T(8,128)} fusion(f32[1024,5,512]{2,1,0:T(8,128)} %gather_fusion.3, pred[1024]{0:T(1024)(128)(4,1)S(1)} %copy-done.37), kind=kLoop, calls=%fused_computation.11 | loop fusion | flops 2621440 | bytes 20972544 | tf_op jit(solution)/shard_map/jit(_take)/select_n | solution.py:176
  247.1 14.8 %copy.222 = f32[5,512,1024]{2,1,0:T(8,128)} copy(f32[5,512,1024]{1,0,2:T(8,128)} %select_bitcast_fusion.3) | data formatting | bytes 20971520 | tf_op jit(solution)/shard_map/jit(_take)/select_n | solution.py:176
  261.9 7.8 %fusion.3 = f32[5,64,1024]{2,1,0:T(8,128)S(1)} fusion(f32[5,512,1024]{2,1,0:T(8,128)} %copy.222, f32[8,1024]{1,0:T(8,128)S(1)} %get-tuple-element.102), kind=kLoop, calls=%fused_computation.20 | loop fusion | flops 4915200 | bytes 11829248 | tf_op jit(solution)/shard_map/reduce_sum | solution.py:177
  270.2 5.3 collective-permute-start.4
  275.6 13.8 %gather_fusion.2 = f32[1024,5,512]{2,1,0:T(8,128)} fusion(f32[5,512,128]{1,0,2:T(8,128)S(1)} %copy.219, s32[1024]{0:T(1024)} %get-tuple-element.155), kind=kCustom, calls=%fused_computation.clone | custom fusion | bytes 20975616 | tf_op jit(solution)/shard_map/jit(_take)/gather | solution.py:176
  289.3 12.3 %select_bitcast_fusion.4 = f32[5,512,1024]{1,0,2:T(8,128)} fusion(f32[1024,5,512]{2,1,0:T(8,128)} %gather_fusion.2, pred[1024]{0:T(1024)(128)(4,1)S(1)} %copy-done.36), kind=kLoop, calls=%fused_computation.12 | loop fusion | flops 2621440 | bytes 20972544 | tf_op jit(solution)/shard_map/jit(_take)/select_n | solution.py:176
  301.6 14.8 %copy.220 = f32[5,512,1024]{2,1,0:T(8,128)} copy(f32[5,512,1024]{1,0,2:T(8,128)} %select_bitcast_fusion.4) | data formatting | bytes 20971520 | tf_op jit(solution)/shard_map/jit(_take)/select_n | solution.py:176
  316.4 7.8 %fusion.4 = f32[5,64,1024]{2,1,0:T(8,128)S(1)} fusion(f32[5,512,1024]{2,1,0:T(8,128)} %copy.220, f32[8,1024]{1,0:T(8,128)S(1)} %get-tuple-element.105), kind=kLoop, calls=%fused_computation.22 | loop fusion | flops 4915200 | bytes 11829248 | tf_op jit(solution)/shard_map/reduce_sum | solution.py:177
  324.7 5.7 collective-permute-start.2
  330.5 7.8 %fusion.2 = f32[5,64,1024]{2,1,0:T(8,128)S(1)} fusion(f32[5,512,1024]{2,1,0:T(8,128)} %copy.224, f32[8,1024]{1,0:T(8,128)S(1)} %get-tuple-element.66), kind=kLoop, calls=%fused_computation.18 | loop fusion | flops 4915200 | bytes 11829248 | tf_op jit(solution)/shard_map/reduce_sum | solution.py:177
  340.5 1.3 collective-permute-done.9
  342.6 7.6 %gather_fusion.1 = f32[2048,5]{1,0:T(8,128)} fusion(f32[5,5120]{0,1:T(8,128)S(1)} %copy.229, s32[2048]{0:T(1024)S(1)} %broadcast_clamp_fusion), kind=kCustom, calls=%fused_computation.6 | custom fusion | bytes 90112 | tf_op jit(solution)/shard_map/jit(_take)/gather | solution.py:189
  350.2 1.6 select_bitcast_fusion.6
  357.2 5.2 collective-permute-start.10
  362.4 3.7 collective-permute-done.10
  366.2 1.5 collective-permute-start.11
  367.7 6.5 %collective-permute-done.11 = f32[1,40960]{1,0:T(1,128)S(1)} collective-permute-done((f32[1,40960]{1,0:T(1,128)S(1)}, f32[1,40960]{1,0:T(1,128)S(1)}, u32[]{:S(2)}, u32[]{:S(2)}) %collective-permute-start.11) | collective-permute-done | bytes 163872 | tf_op jit(solution)/shard_map/ppermute | solution.py:24
  378.7 4.5 collective-permute-start.12
  383.2 1.6 collective-permute-done.12
  386.1 4.8 collective-permute-done.13
  395.4 4.8 collective-permute-start.14
  400.2 1.6 collective-permute-done.14
  403.1 4.8 collective-permute-done.15
  408.7 41.1 %all-reduce.2 = (f32[]{:T(128)}, f32[]{:T(128)}) all-reduce(f32[]{:T(128)} %get-tuple-element.25, f32[]{:T(128)} %get-tuple-element.24), channel_id=1, replica_groups=mesh['mesh'=2,'dom'=16] {'dom'}, use_global_device_ids=true, to_apply=%region_21.24 | all-reduce | flops 2 | bytes 16 | tf_op jit(solution)/shard_map/psum | solution.py:230
  455.8 1.3 collective-permute-start.16
  457.1 1.6 collective-permute-done.16
  460.0 4.8 collective-permute-done.17
  464.8 1.4 fusion.96
  466.3 40.4 %all-reduce.1 = (f32[]{:T(128)}, f32[]{:T(128)}) all-reduce(f32[]{:T(128)} %get-tuple-element.23, f32[]{:T(128)} %get-tuple-element.22), channel_id=1, replica_groups=mesh['mesh'=2,'dom'=16] {'dom'}, use_global_device_ids=true, to_apply=%region_25.28 | all-reduce | flops 2 | bytes 16 | tf_op jit(solution)/shard_map/psum | solution.py:230
  511.2 1.8 bitcast_multiply_fusion.18
  518.1 1.6 collective-permute-done.18
  522.5 4.1 collective-permute-done.19
  528.0 1.8 fusion.97
  529.8 40.1 %all-reduce = (f32[]{:T(128)}, f32[]{:T(128)}) all-reduce(f32[]{:T(128)} %get-tuple-element.21, f32[]{:T(128)} %get-tuple-element.20), channel_id=1, replica_groups=mesh['mesh'=2,'dom'=16] {'dom'}, use_global_device_ids=true, to_apply=%region_29.32 | all-reduce | flops 2 | bytes 16 | tf_op jit(solution)/shard_map/psum | solution.py:230
  (274 shorter events, 55.2 us)
Async XLA Ops:
  36.8 2.9 copy-start.42
  36.8 2.9 copy-start.41
  37.8 5.2 copy-start.33
  37.8 5.2 copy-start.34
  37.8 18.6 %collective-permute-start = (f32[25,5120]{1,0:T(8,128)S(1)}, f32[25,5120]{1,0:T(8,128)}, u32[]{:S(2)}, u32[]{:S(2)}) collective-permute-start(f32[25,5120]{1,0:T(8,128)S(1)} %copy.218), channel_id=1, source_target_pairs={{0,16},{16,0},{1,17},{17,1},{2,18},{18,2},{3,19},{19,3},{4,20},{20... | collective-permute-start | bytes 1536008 | tf_op jit(solution)/shard_map/ppermute | solution.py:36
  38.4 20.6 %copy-start.22 = (pred[128]{0:T(512)(128)(4,1)}, pred[128]{0:T(512)(128)(4,1)S(1)}, u32[]{:S(2)}) copy-start(pred[128]{0:T(512)(128)(4,1)S(1)} %broadcast_compare_fusion.5) | copy-start | bytes 388
  38.4 20.6 %copy-start.27 = (pred[128]{0:T(512)(128)(4,1)}, pred[128]{0:T(512)(128)(4,1)S(1)}, u32[]{:S(2)}) copy-start(pred[128]{0:T(512)(128)(4,1)S(1)} %broadcast_compare_fusion.1) | copy-start | bytes 388
  59.0 11.9 %collective-permute-start.7 = (f32[25,1024]{1,0:T(8,128)S(1)}, f32[25,1024]{1,0:T(8,128)S(1)}, u32[]{:S(2)}, u32[]{:S(2)}) collective-permute-start(f32[25,1024]{1,0:T(8,128)S(1)} %get-tuple-element.60), channel_id=1, source_target_pairs={{0,2},{1,3},{2,4},{3,5},{4,6},{5,7},{6,8},{7,9},{8,10},{9,11},{10,... | collective-permute-start | bytes 307208 | tf_op jit(solution)/shard_map/ppermute | solution.py:42
  63.4 7.5 %collective-permute-start.5 = (f32[25,1024]{1,0:T(8,128)S(1)}, f32[25,1024]{1,0:T(8,128)S(1)}, u32[]{:S(2)}, u32[]{:S(2)}) collective-permute-start(f32[25,1024]{1,0:T(8,128)S(1)} %get-tuple-element.61), channel_id=1, source_target_pairs={{0,1},{1,2},{2,3},{3,4},{4,5},{5,6},{6,7},{7,8},{8,9},{9,10},{10,1... | collective-permute-start | bytes 307208 | tf_op jit(solution)/shard_map/ppermute | solution.py:42
  66.9 7.8 %collective-permute-start.3 = (f32[25,1024]{1,0:T(8,128)S(1)}, f32[25,1024]{1,0:T(8,128)S(1)}, u32[]{:S(2)}, u32[]{:S(2)}) collective-permute-start(f32[25,1024]{1,0:T(8,128)S(1)} %get-tuple-element.62), channel_id=1, source_target_pairs={{1,0},{2,1},{3,2},{4,3},{5,4},{6,5},{7,6},{8,7},{9,8},{10,9},{11,1... | collective-permute-start | bytes 307208 | tf_op jit(solution)/shard_map/ppermute | solution.py:42
  68.2 8.8 %collective-permute-start.1 = (f32[25,1024]{1,0:T(8,128)S(1)}, f32[25,1024]{1,0:T(8,128)S(1)}, u32[]{:S(2)}, u32[]{:S(2)}) collective-permute-start(f32[25,1024]{1,0:T(8,128)S(1)} %get-tuple-element.63), channel_id=1, source_target_pairs={{2,0},{3,1},{4,2},{5,3},{6,4},{7,5},{8,6},{9,7},{10,8},{11,9},{12,... | collective-permute-start | bytes 307208 | tf_op jit(solution)/shard_map/ppermute | solution.py:42
  70.9 20.8 %copy-start.14 = (f32[25,1024]{1,0:T(8,128)}, f32[25,1024]{1,0:T(8,128)S(1)}, u32[]{:S(2)}) copy-start(f32[25,1024]{1,0:T(8,128)S(1)} %collective-permute-done.5) | copy-start | bytes 307204
  74.7 17.1 %copy-start.12 = (f32[25,1024]{1,0:T(8,128)}, f32[25,1024]{1,0:T(8,128)S(1)}, u32[]{:S(2)}) copy-start(f32[25,1024]{1,0:T(8,128)S(1)} %collective-permute-done.3) | copy-start | bytes 307204
  76.9 14.9 %copy-start.10 = (f32[25,1024]{1,0:T(8,128)}, f32[25,1024]{1,0:T(8,128)S(1)}, u32[]{:S(2)}) copy-start(f32[25,1024]{1,0:T(8,128)S(1)} %collective-permute-done.1) | copy-start | bytes 307204
  127.7 212.0 %collective-permute-start.8 = (f32[5,1024]{1,0:T(8,128)}, f32[5,1024]{1,0:T(8,128)}, u32[]{:S(2)}, u32[]{:S(2)}) collective-permute-start(f32[5,1024]{1,0:T(8,128)} %multiply_reduce_fusion), channel_id=1, source_target_pairs={{2,0},{3,1},{4,2},{5,3},{6,4},{7,5},{8,6},{9,7},{10,8},{11,9},{12,... | collective-permute-start | bytes 61448 | tf_op jit(solution)/shard_map/ppermute | solution.py:42
  129.2 13.8 %copy-start.38 = (pred[1024]{0:T(1024)(128)(4,1)S(1)}, pred[1024]{0:T(1024)(128)(4,1)}, u32[]{:S(2)}) copy-start(pred[1024]{0:T(1024)(128)(4,1)} %compare_and_fusion.2) | copy-start | bytes 3076
  155.3 14.7 %copy-start.15 = (f32[25,1024]{1,0:T(8,128)S(1)}, f32[25,1024]{1,0:T(8,128)}, u32[]{:S(2)}) copy-start(f32[25,1024]{1,0:T(8,128)} %copy-done.14) | copy-start | bytes 307204
  178.9 160.0 %collective-permute-start.6 = (f32[5,1024]{1,0:T(8,128)}, f32[5,1024]{1,0:T(8,128)}, u32[]{:S(2)}, u32[]{:S(2)}) collective-permute-start(f32[5,1024]{1,0:T(8,128)} %multiply_reduce_fusion.1), channel_id=1, source_target_pairs={{1,0},{2,1},{3,2},{4,3},{5,4},{6,5},{7,6},{8,7},{9,8},{10,9},{11,1... | collective-permute-start | bytes 61448 | tf_op jit(solution)/shard_map/ppermute | solution.py:42
  180.4 13.8 %copy-start.35 = (pred[1024]{0:T(1024)(128)(4,1)S(1)}, pred[1024]{0:T(1024)(128)(4,1)}, u32[]{:S(2)}) copy-start(pred[1024]{0:T(1024)(128)(4,1)} %compare_and_fusion.3) | copy-start | bytes 3076
  206.5 14.7 %copy-start.21 = (s32[1024]{0:T(1024)S(1)}, s32[1024]{0:T(1024)}, u32[]{:S(2)}) copy-start(s32[1024]{0:T(1024)} %get-tuple-element.156) | copy-start | bytes 12292
  221.2 13.6 %copy-start.37 = (pred[1024]{0:T(1024)(128)(4,1)S(1)}, pred[1024]{0:T(1024)(128)(4,1)}, u32[]{:S(2)}) copy-start(pred[1024]{0:T(1024)(128)(4,1)} %compare_and_fusion.4) | copy-start | bytes 3076
  247.1 14.8 %copy-start.13 = (f32[25,1024]{1,0:T(8,128)S(1)}, f32[25,1024]{1,0:T(8,128)}, u32[]{:S(2)}) copy-start(f32[25,1024]{1,0:T(8,128)} %copy-done.12) | copy-start | bytes 307204
  270.2 68.6 %collective-permute-start.4 = (f32[5,1024]{1,0:T(8,128)S(1)}, f32[5,1024]{1,0:T(8,128)S(1)}, u32[]{:S(2)}, u32[]{:S(2)}) collective-permute-start(f32[5,1024]{1,0:T(8,128)S(1)} %multiply_reduce_fusion.3), channel_id=1, source_target_pairs={{0,1},{1,2},{2,3},{3,4},{4,5},{5,6},{6,7},{7,8},{8,9},{9,10},{10,1... | collective-permute-start | bytes 61448 | tf_op jit(solution)/shard_map/ppermute | solution.py:42
  275.6 13.8 %copy-start.36 = (pred[1024]{0:T(1024)(128)(4,1)S(1)}, pred[1024]{0:T(1024)(128)(4,1)}, u32[]{:S(2)}) copy-start(pred[1024]{0:T(1024)(128)(4,1)} %compare_and_fusion.5) | copy-start | bytes 3076
  301.6 14.8 %copy-start.11 = (f32[25,1024]{1,0:T(8,128)S(1)}, f32[25,1024]{1,0:T(8,128)}, u32[]{:S(2)}) copy-start(f32[25,1024]{1,0:T(8,128)} %copy-done.10) | copy-start | bytes 307204
  324.7 14.1 %collective-permute-start.2 = (f32[5,1024]{1,0:T(8,128)S(1)}, f32[5,1024]{1,0:T(8,128)S(1)}, u32[]{:S(2)}, u32[]{:S(2)}) collective-permute-start(f32[5,1024]{1,0:T(8,128)S(1)} %multiply_reduce_fusion.4), channel_id=1, source_target_pairs={{0,2},{1,3},{2,4},{3,5},{4,6},{5,7},{6,8},{7,9},{8,10},{9,11},{10,... | collective-permute-start | bytes 61448 | tf_op jit(solution)/shard_map/ppermute | solution.py:42
  330.4 7.9 %copy-start.9 = (f32[8,1024]{1,0:T(8,128)S(1)}, f32[8,1024]{1,0:T(8,128)}, u32[]{:S(2)}) copy-start(f32[8,1024]{1,0:T(8,128)} %get-tuple-element.65) | copy-start | bytes 98308
  330.4 8.3 %copy-start.8 = (f32[8,1024]{1,0:T(8,128)S(1)}, f32[8,1024]{1,0:T(8,128)}, u32[]{:S(2)}) copy-start(f32[8,1024]{1,0:T(8,128)} %get-tuple-element.64) | copy-start | bytes 98308
  330.4 10.0 %copy-start.28 = (pred[128]{0:T(512)(128)(4,1)S(1)}, pred[128]{0:T(512)(128)(4,1)}, u32[]{:S(2)}) copy-start(pred[128]{0:T(512)(128)(4,1)} %copy-done.27) | copy-start | bytes 388
  330.5 10.0 %copy-start.43 = (pred[8]{0:T(512)(128)(4,1)S(1)}, pred[8]{0:T(512)(128)(4,1)}, u32[]{:S(2)}) copy-start(pred[8]{0:T(512)(128)(4,1)} %slice.536) | copy-start | bytes 28
  338.7 11.5 %copy-start.32 = (pred[2048]{0:T(1024)(128)(4,1)S(1)}, pred[2048]{0:T(1024)(128)(4,1)}, u32[]{:S(2)}) copy-start(pred[2048]{0:T(1024)(128)(4,1)} %get-tuple-element.50) | copy-start | bytes 6148
  340.4 1.4 collective-permute-start.9
  340.5 16.3 %copy-start.30 = (pred[128]{0:T(512)(128)(4,1)}, pred[128]{0:T(512)(128)(4,1)S(1)}, u32[]{:S(2)}) copy-start(pred[128]{0:T(512)(128)(4,1)S(1)} %pad_add_fusion) | copy-start | bytes 388
  351.8 1.6 copy-start.39
  351.8 1.6 copy-start.40
  351.8 1.6 copy-start.20
  351.8 1.7 copy-start.19
  351.8 1.7 copy-start.7
  351.8 1.7 copy-start.17
  351.8 1.7 copy-start.18
  353.5 1.5 copy-start.23
  353.6 1.5 copy-start.25
  357.2 8.9 %collective-permute-start.10 = (f32[1,40960]{1,0:T(1,128)S(1)}, f32[1,40960]{1,0:T(1,128)S(1)}, u32[]{:S(2)}, u32[]{:S(2)}) collective-permute-start(f32[1,40960]{1,0:T(1,128)S(1)} %bitcast.397), channel_id=1, source_target_pairs={{0,1},{1,2},{2,3},{3,4},{4,5},{5,6},{6,7},{7,8},{8,9},{9,10},{10,1... | collective-permute-start | bytes 491528 | tf_op jit(solution)/shard_map/ppermute | solution.py:23
  366.2 8.0 %collective-permute-start.11 = (f32[1,40960]{1,0:T(1,128)S(1)}, f32[1,40960]{1,0:T(1,128)S(1)}, u32[]{:S(2)}, u32[]{:S(2)}) collective-permute-start(f32[1,40960]{1,0:T(1,128)S(1)} %bitcast.400), channel_id=1, source_target_pairs={{1,0},{2,1},{3,2},{4,3},{5,4},{6,5},{7,6},{8,7},{9,8},{10,9},{11,1... | collective-permute-start | bytes 491528 | tf_op jit(solution)/shard_map/ppermute | solution.py:24
  374.2 0.7 copy-start.4
  374.4 2.8 copy-start.1
  374.4 2.8 copy-start.5
  375.9 2.4 copy-start.31
  376.3 2.1 copy-start.29
  378.7 6.1 %collective-permute-start.12 = (f32[1,8192]{1,0:T(1,128)S(1)}, f32[1,8192]{1,0:T(1,128)S(1)}, u32[]{:S(2)}, u32[]{:S(2)}) collective-permute-start(f32[1,8192]{1,0:T(1,128)S(1)} %bitcast.404), channel_id=1, source_target_pairs={{0,1},{1,2},{2,3},{3,4},{4,5},{5,6},{6,7},{7,8},{8,9},{9,10},{10,1... | collective-permute-start | bytes 98312 | tf_op jit(solution)/shard_map/ppermute | solution.py:23
  384.8 6.1 %collective-permute-start.13 = (f32[1,8192]{1,0:T(1,128)S(1)}, f32[1,8192]{1,0:T(1,128)S(1)}, u32[]{:S(2)}, u32[]{:S(2)}) collective-permute-start(f32[1,8192]{1,0:T(1,128)S(1)} %bitcast.430), channel_id=1, source_target_pairs={{1,0},{2,1},{3,2},{4,3},{5,4},{6,5},{7,6},{8,7},{9,8},{10,9},{11,1... | collective-permute-start | bytes 98312 | tf_op jit(solution)/shard_map/ppermute | solution.py:24
  395.4 6.4 %collective-permute-start.14 = (f32[1,8192]{1,0:T(1,128)S(1)}, f32[1,8192]{1,0:T(1,128)S(1)}, u32[]{:S(2)}, u32[]{:S(2)}) collective-permute-start(f32[1,8192]{1,0:T(1,128)S(1)} %bitcast.405), channel_id=1, source_target_pairs={{0,1},{1,2},{2,3},{3,4},{4,5},{5,6},{6,7},{7,8},{8,9},{9,10},{10,1... | collective-permute-start | bytes 98312 | tf_op jit(solution)/shard_map/ppermute | solution.py:23
  401.8 6.1 %collective-permute-start.15 = (f32[1,8192]{1,0:T(1,128)S(1)}, f32[1,8192]{1,0:T(1,128)S(1)}, u32[]{:S(2)}, u32[]{:S(2)}) collective-permute-start(f32[1,8192]{1,0:T(1,128)S(1)} %bitcast.431), channel_id=1, source_target_pairs={{1,0},{2,1},{3,2},{4,3},{5,4},{6,5},{7,6},{8,7},{9,8},{10,9},{11,1... | collective-permute-start | bytes 98312 | tf_op jit(solution)/shard_map/ppermute | solution.py:24
  453.3 1.9 copy-start.24
  453.3 1.9 copy-start.26
  455.8 2.9 collective-permute-start.16
  458.7 6.1 %collective-permute-start.17 = (f32[1,8192]{1,0:T(1,128)S(1)}, f32[1,8192]{1,0:T(1,128)S(1)}, u32[]{:S(2)}, u32[]{:S(2)}) collective-permute-start(f32[1,8192]{1,0:T(1,128)S(1)} %bitcast.432), channel_id=1, source_target_pairs={{1,0},{2,1},{3,2},{4,3},{5,4},{6,5},{7,6},{8,7},{9,8},{10,9},{11,1... | collective-permute-start | bytes 98312 | tf_op jit(solution)/shard_map/ppermute | solution.py:24
  516.7 2.9 copy-start
  516.8 3.5 copy-start.6
  516.8 2.9 collective-permute-start.18
  520.3 6.3 %collective-permute-start.19 = (f32[1,8192]{1,0:T(1,128)}, f32[1,8192]{1,0:T(1,128)S(1)}, u32[]{:S(2)}, u32[]{:S(2)}) collective-permute-start(f32[1,8192]{1,0:T(1,128)} %bitcast.118), channel_id=1, source_target_pairs={{1,0},{2,1},{3,2},{4,3},{5,4},{6,5},{7,6},{8,7},{9,8},{10,9},{11,1... | collective-permute-start | bytes 98312 | tf_op jit(solution)/shard_map/ppermute | solution.py:24
  522.5 52.4 %copy-start.2 = (f32[1,8,8,8,128]{4,3,2,1,0:T(8,128)S(1)}, f32[1,8,8,8,128]{4,3,2,1,0:T(8,128)}, u32[]{:S(2)}) copy-start(f32[1,8,8,8,128]{4,3,2,1,0:T(8,128)} %copy-done.1) | copy-start | bytes 786436
  522.5 52.4 %copy-start.3 = (f32[1,8,8,8,128]{4,3,2,1,0:T(8,128)S(1)}, f32[1,8,8,8,128]{4,3,2,1,0:T(8,128)}, u32[]{:S(2)}) copy-start(f32[1,8,8,8,128]{4,3,2,1,0:T(8,128)} %get-tuple-element.44) | copy-start | bytes 786436
  526.6 0.6 copy-start.16
where the time goes:
time: 587 us; the launch traced here: 576 us
  local copies, waits for them, and re-layouts  193 us (33%)
  other arithmetic  150 us (26%)
  blocking collectives  122 us (21%)
  starting transfers between devices  48.8 us (8%)
  waiting for transfers between devices  40.6 us (7%)
  between operations  12.5 us (2%)
  matrix products  10.3 us (2%)
    psum x3, blocking collectives, paired_dots(): lax.psum((jnp.sum(residual_now * precond / multiplicity), jnp.sum(precond...  122 us
    select_n x5, local copies, waits for them, and re-layouts, body(): jnp.take(donor_fields, lookups, axis=2).reshape(field_count, 64, 8, count)  73.5 us
    gather x5, local copies, waits for them, and re-layouts, body(): jnp.take(donor_fields, lookups, axis=2).reshape(field_count, 64, 8, count)  68.5 us
    select_n x5, other arithmetic, body(): jnp.take(donor_fields, lookups, axis=2).reshape(field_count, 64, 8, count)  61.6 us
    reduce_sum x5, other arithmetic, body(): jnp.sum(gathered * piece[0:8][None, None], axis=2)  39.1 us
    ppermute x5, waiting for transfers between devices, with_halo(): after = lax.ppermute(leading, axis, down)  25 us
    ppermute x8, starting transfers between devices, from_behind(): lax.ppermute(value, axis, [(source, source + steps) for source in range(l...  24.5 us
    gather x1, local copies, waits for them, and re-layouts, body(): outgoing = jnp.take(packed, source_row, axis=1)  17.7 us
  transfers between devices with their start and end apart: 20, of which 13 were waited for; matrix products, arithmetic and copies ran while one was open for 38% of the time, Pallas kernels for 0%

commit v1 on v0

v1 whole, which is shorter than its diff:
```python
import functools

import jax
import jax.numpy as jnp
import numpy as np
from jax import lax
from jax.experimental import pallas as pl
from jax.experimental.pallas import tpu as pltpu
from jax.sharding import PartitionSpec as P

EX = 8
EY = 16
ITERS = 3
REACH = 2
CHUNK = 256
ORDER = (0, 7, 1, 2, 3, 4, 5, 6)
MESH = pl.DeviceIdType.MESH


def legendre_pair(values, degree):
    previous = values * 0.0 + 1.0
    current = values * 1.0
    for poly_order in range(2, degree + 1):
        previous, current = (
            current,
            ((2 * poly_order - 1) * values * current - (poly_order - 1) * previous) / poly_order,
        )
    return (current, previous)


def gll_tables():
    degree = 7
    points_count = degree + 1
    abscissae = np.cos(np.pi * np.arange(points_count) / degree)
    for newton_turn in range(80):
        top_poly, lower_poly = legendre_pair(abscissae, degree)
        abscissae = abscissae - (abscissae * top_poly - lower_poly) / (points_count * top_poly)
    abscissae = np.sort(abscissae)
    top_poly, lower_poly = legendre_pair(abscissae, degree)
    quad_weights = 2.0 / (degree * points_count * top_poly * top_poly)
    identity_mat = np.eye(points_count)
    spacing = abscissae[:, None] - abscissae[None, :] + identity_mat
    derivative = top_poly[:, None] / (top_poly[None, :] * spacing) * (1.0 - identity_mat)
    derivative[0, 0] = -degree * points_count / 4.0
    derivative[degree, degree] = degree * points_count / 4.0
    return (abscissae, derivative, quad_weights)


def kernel(
    n,
    request_ref,
    donor_ref,
    geometry_ref,
    wall_ref,
    forcing_ref,
    along_y_ref,
    along_x_ref,
    plane_ref,
    place_ref,
    velocity_ref,
    residual_ref,
    interface_ref,
    split,
    asked,
    answer,
    answered,
    faces,
    halo,
    dots,
    all_dots,
    state,
    image,
    direction,
    direction_image,
    inverse,
    free,
    sharing,
    boundary,
    ask_send,
    ask_recv,
    reply_send,
    reply_recv,
    face_send,
    face_recv,
    dot_send,
    dot_recv,
):
    points, derivative, quad = gll_tables()
    stiff = (derivative.T * quad) @ derivative / quad[:, None]
    fields = donor_ref.shape[0]
    elems = donor_ref.shape[2]
    receptors = request_ref.shape[1]
    slots = 2 * REACH + 1
    mesh_id = lax.axis_index("mesh")
    slab = lax.axis_index("dom")
    other = 1 - mesh_id

    def inside(index):
        return jnp.logical_and(index >= 0, index < n)

    barrier = pltpu.get_barrier_semaphore()
    greeted = n - 1
    for step in range(1, n):
        pl.semaphore_signal(
            barrier, inc=1, device_id=(mesh_id, lax.rem(slab + step, n)), device_id_type=MESH
        )
    for shift in range(-REACH, REACH + 1):
        greeted = greeted + jnp.where(inside(slab + shift), 1, 0)

        @pl.when(inside(slab + shift))
        def _():
            pl.semaphore_signal(
                barrier, inc=1, device_id=(other, slab + shift), device_id_type=MESH
            )

    pl.semaphore_wait(barrier, greeted)

    def ask(shift):
        return pltpu.make_async_remote_copy(
            src_ref=request_ref,
            dst_ref=asked.at[shift + REACH],
            send_sem=ask_send.at[shift + REACH],
            recv_sem=ask_recv.at[shift + REACH],
            device_id=(other, lax.rem(slab + shift + n, n)),
            device_id_type=MESH,
        )

    def reply(shift):
        return pltpu.make_async_remote_copy(
            src_ref=answer.at[shift + REACH],
            dst_ref=answered.at[shift + REACH],
            send_sem=reply_send.at[shift + REACH],
            recv_sem=reply_recv.at[shift + REACH],
            device_id=(other, lax.rem(slab - shift + n, n)),
            device_id_type=MESH,
        )

    def face_copy(phase, up):
        step = 1 if up else n - 1
        return pltpu.make_async_remote_copy(
            src_ref=faces.at[phase, 1 if up else 0],
            dst_ref=halo.at[phase, 0 if up else 1],
            send_sem=face_send.at[phase, 1 if up else 0],
            recv_sem=face_recv.at[phase, 0 if up else 1],
            device_id=(mesh_id, lax.rem(slab + step, n)),
            device_id_type=MESH,
        )

    def send_faces(phase):
        @pl.when(slab < n - 1)
        def _():
            face_copy(phase, True).start()

        @pl.when(slab > 0)
        def _():
            face_copy(phase, False).start()

    def wait_faces(phase):
        @pl.when(slab > 0)
        def _():
            face_copy(phase, True).wait_recv()

        @pl.when(slab < n - 1)
        def _():
            face_copy(phase, False).wait_recv()

        @pl.when(slab < n - 1)
        def _():
            face_copy(phase, True).wait_send()

        @pl.when(slab > 0)
        def _():
            face_copy(phase, False).wait_send()

    def dot_copy(turn, step):
        return pltpu.make_async_remote_copy(
            src_ref=dots.at[turn],
            dst_ref=all_dots.at[turn, slab],
            send_sem=dot_send.at[turn, step],
            recv_sem=dot_recv.at[turn, step],
            device_id=(mesh_id, lax.rem(slab + step, n)),
            device_id_type=MESH,
        )

    for distance in range(REACH + 1):
        for shift in sorted({distance, -distance}):

            @pl.when(inside(slab + shift))
            def _():
                ask(shift).start()

    phases = halo.shape[0]
    blank = jnp.zeros(halo.shape[2:], jnp.float32)

    @pl.when(slab == 0)
    def _():
        for phase in range(phases):
            halo[phase, 0] = blank

    @pl.when(slab == n - 1)
    def _():
        for phase in range(phases):
            halo[phase, 1] = blank

    node = lax.broadcasted_iota(jnp.int32, (8, elems), 0)
    element = lax.broadcasted_iota(jnp.int32, (8, elems), 1)
    x_index = element % EX
    y_index = element // EX % EY

    def flag(condition):
        return jnp.where(condition, 1.0, 0.0)

    x_low = flag((node == 0) & (x_index > 0))
    x_high = flag((node == 7) & (x_index < EX - 1))
    y_low = flag(y_index > 0)
    y_high = flag(y_index < EY - 1)

    def plane_sum(tile):
        below = pltpu.roll(pltpu.roll(tile, 1, 1), 1, 2)
        above = pltpu.roll(pltpu.roll(tile, 7, 1), elems - 1, 2)
        tile = tile + below * x_low + above * x_high
        low = tile[0] + y_low * pltpu.roll(tile[7], EX, 1)
        high = tile[7] + y_high * pltpu.roll(tile[0], elems - EX, 1)
        return jnp.concatenate([low[None], tile[1:7], high[None]], 0)

    def weights(layer):
        return plane_ref[...] * float(quad[layer])

    g_x, g_y, g_z, g_m = [geometry_ref[d : d + 1, :] for d in range(4)]

    diag_plane = jnp.zeros((8, 8, elems), jnp.float32) + g_m
    diag_plane = diag_plane + g_x * along_x_ref[0]
    diag_plane = diag_plane + jnp.concatenate(
        [(g_y * float(stiff[j, j]) + jnp.zeros((8, elems), jnp.float32))[None] for j in range(8)], 0
    )
    for layer in ORDER:
        image[layer] = plane_sum(
            weights(layer) * (diag_plane + g_z * float(stiff[layer, layer]))
        )
    wall_low = flag(y_index == 0) * wall_ref[0:1, :]
    wall_high = flag(y_index == EY - 1) * wall_ref[1:2, :]
    nothing = jnp.zeros((6, 8, elems), jnp.float32)
    wall_plane = plane_sum(jnp.concatenate([wall_low[None], nothing, wall_high[None]], 0))
    faces[0, 0] = image[0]
    faces[0, 1] = image[7]
    faces[1, 0] = wall_plane
    faces[1, 1] = wall_plane
    send_faces(0)
    send_faces(1)

    donors = donor_ref[...].reshape(fields * 512, elems)
    coarse = donors.astype(jnp.bfloat16)
    split[:, :elems] = coarse
    split[:, elems:] = (donors - coarse.astype(jnp.float32)).astype(jnp.bfloat16)

    code = lax.broadcasted_iota(jnp.int32, (elems, CHUNK), 0) + slab * elems
    code = code.astype(jnp.float32)
    basis = lax.broadcasted_iota(jnp.int32, (8, CHUNK), 0)
    norms = [
        float(1.0 / np.prod([points[a] - points[b] for b in range(8) if b != a])) for a in range(8)
    ]
    scale = jnp.zeros((8, CHUNK), jnp.float32)
    for a in range(8):
        scale = jnp.where(basis == a, norms[a], scale)

    def lagrange(position):
        value = scale
        for b in range(8):
            value = value * jnp.where(basis == b, 1.0, position - float(points[b]))
        return value

    def serve(turn, carry):
        shift = ((turn + 1) // 2) * (2 * (turn % 2) - 1)

        @pl.when(inside(slab - shift))
        def _():
            ask(shift).wait_recv()

            def part(chunk, carry):
                block = asked[shift + REACH, :, pl.ds(pl.multiple_of(chunk * CHUNK, CHUNK), CHUNK)]
                chosen = jnp.where(block[3:4, :] == code, 1.0, 0.0).astype(jnp.bfloat16)
                chosen = jnp.concatenate([chosen, chosen], 0)
                w_x, w_y, w_z = [lagrange(block[d : d + 1, :]) for d in range(3)]
                found = jnp.dot(split[...], chosen, preferred_element_type=jnp.float32)
                for field in range(fields):
                    cube = found[field * 512 : (field + 1) * 512].reshape(8, 64, CHUNK)
                    total = cube[0] * w_z[0:1, :]
                    for k in range(1, 8):
                        total = total + cube[k] * w_z[k : k + 1, :]
                    total = total.reshape(8, 8, CHUNK)
                    line = total[0] * w_y[0:1, :]
                    for j in range(1, 8):
                        line = line + total[j] * w_y[j : j + 1, :]
                    answer[shift + REACH, field, pl.ds(chunk, 1), :] = jnp.sum(
                        line * w_x, axis=0, keepdims=True
                    )
                return carry

            lax.fori_loop(0, receptors // CHUNK, part, 0)
            reply(shift).start()

        return carry

    lax.fori_loop(0, slots, serve, 0)

    z_low = jnp.where(slab > 0, 2.0, 1.0)
    z_high = jnp.where(slab < n - 1, 2.0, 1.0)
    x_count = 1.0 + x_low + x_high
    y_count_low = 1.0 + y_low
    y_count_high = 1.0 + y_high
    plane_count = jnp.concatenate(
        [(x_count * y_count_low)[None]]
        + [x_count[None]] * 6
        + [(x_count * y_count_high)[None]],
        0,
    )
    mark = flag((node == 0) & (x_index == 0)) + flag((node == 7) & (x_index == EX - 1))
    wait_faces(0)
    wait_faces(1)
    image[0] = image[0] + halo[0, 0]
    image[7] = image[7] + halo[0, 1]
    for layer in range(8):
        count = plane_count
        walls = wall_plane
        if layer == 0:
            count = count * z_low
            walls = walls + halo[1, 0]
        if layer == 7:
            count = count * z_high
            walls = walls + halo[1, 1]
        open_part = 1.0 - jnp.minimum(mark * count + walls, 1.0)
        sharing[layer] = 1.0 / count
        free[layer] = open_part
        inverse[layer] = open_part / image[layer]

    interface_sum = jnp.zeros((fields, receptors // CHUNK, CHUNK), jnp.float32)
    for shift in range(-REACH, REACH + 1):

        @pl.when(jnp.logical_not(inside(slab + shift)))
        def _():
            answered[shift + REACH] = jnp.zeros(answered.shape[1:], jnp.float32)

        @pl.when(inside(slab + shift))
        def _():
            reply(shift).wait_recv()

    for shift in range(-REACH, REACH + 1):
        interface_sum = interface_sum + answered[shift + REACH]
    for chunk in range(receptors // CHUNK):
        interface_ref[:, chunk * CHUNK : (chunk + 1) * CHUNK] = interface_sum[:, chunk, :]

    rows = interface_sum[0]
    groups = CHUNK // 64
    rows = jnp.concatenate([rows[:, t * 64 : (t + 1) * 64] for t in range(groups)], 0)
    placed = lax.dot_general(
        rows,
        place_ref[...],
        (((0,), (0,)), ((), ())),
        precision=lax.Precision.HIGHEST,
        preferred_element_type=jnp.float32,
    ).reshape(8, 8, elems)
    for layer in ORDER:
        spread = jnp.concatenate(
            [(jnp.broadcast_to(placed[layer, j : j + 1, :], (8, elems)) * mark)[None] for j in range(8)],
            0,
        )
        boundary[layer] = plane_sum(spread)
        if layer == 7:
            faces[2, 0] = boundary[0]
            faces[2, 1] = boundary[7]
            send_faces(2)
    wait_faces(2)
    boundary[0] = boundary[0] + halo[2, 0]
    boundary[7] = boundary[7] + halo[2, 1]
    for layer in range(8):
        boundary[layer] = boundary[layer] * sharing[layer]

    def local_tile(source, layer):
        tile = source[layer]
        along_z = source[0] * float(stiff[layer, 0])
        for k in range(1, 8):
            along_z = along_z + source[k] * float(stiff[layer, k])
        along_y = along_y_ref[0] * tile[0:1]
        for j in range(1, 8):
            along_y = along_y + along_y_ref[j] * tile[j : j + 1]
        along_x = along_x_ref[0] * tile
        for step in range(1, 8):
            along_x = along_x + along_x_ref[step] * pltpu.roll(tile, step, 1)
        total = g_x * along_x + g_y * along_y + g_z * along_z + g_m * tile
        return weights(layer) * total

    for layer in ORDER:
        loaded = weights(layer) * g_m * forcing_ref[layer] - local_tile(boundary, layer)
        residual_ref[layer] = plane_sum(loaded)
        if layer == 7:
            faces[3, 0] = residual_ref[0]
            faces[3, 1] = residual_ref[7]
            send_faces(3)
    wait_faces(3)
    residual_ref[0] = residual_ref[0] + halo[3, 0]
    residual_ref[7] = residual_ref[7] + halo[3, 1]
    for layer in range(8):
        residual_ref[layer] = residual_ref[layer] * free[layer]
        velocity_ref[layer] = boundary[layer]
        direction[layer] = jnp.zeros((8, 8, elems), jnp.float32)
        direction_image[layer] = jnp.zeros((8, 8, elems), jnp.float32)

    def iterate(turn, carry):
        norm, length = carry
        phase = turn + 4
        norm_part = jnp.zeros((8, 8, elems), jnp.float32)
        for layer in range(8):
            state[layer] = inverse[layer] * residual_ref[layer]
            norm_part = norm_part + state[layer] * residual_ref[layer] * sharing[layer]
        curve_part = jnp.zeros((8, 8, elems), jnp.float32)
        for layer in ORDER:
            tile = local_tile(state, layer)
            curve_part = curve_part + tile * state[layer]
            image[layer] = plane_sum(tile)
            if layer == 7:
                faces[phase, 0] = image[0]
                faces[phase, 1] = image[7]
                send_faces(phase)
        dots[turn, 0:1, :] = jnp.sum(jnp.sum(norm_part, axis=0), axis=0, keepdims=True)
        dots[turn, 1:2, :] = jnp.sum(jnp.sum(curve_part, axis=0), axis=0, keepdims=True)
        for step in range(1, n):
            dot_copy(turn, step).start()
        all_dots[turn, slab] = dots[turn]
        wait_faces(phase)
        image[0] = image[0] + halo[phase, 0]
        image[7] = image[7] + halo[phase, 1]
        for step in range(1, n):
            dot_copy(turn, step).wait_recv()
        sums = jnp.sum(jnp.sum(all_dots[turn], axis=0), axis=1, keepdims=True)
        norm_next, curvature = sums[0:1, :], sums[1:2, :]
        ratio = jnp.where(turn == 0, 0.0, norm_next / norm)
        length = norm_next / (curvature - ratio * norm_next / length)
        for layer in range(8):
            toward = state[layer] + ratio * direction[layer]
            toward_image = free[layer] * image[layer] + ratio * direction_image[layer]
            direction[layer] = toward
            direction_image[layer] = toward_image
            velocity_ref[layer] = velocity_ref[layer] + length * toward
            residual_ref[layer] = residual_ref[layer] - length * toward_image
        for step in range(1, n):
            dot_copy(turn, step).wait_send()
        return norm_next, length

    one = jnp.ones((1, 1), jnp.float32)
    lax.fori_loop(0, ITERS, iterate, (one, one))

    for shift in range(-REACH, REACH + 1):

        @pl.when(inside(slab + shift))
        def _():
            ask(shift).wait_send()

        @pl.when(inside(slab - shift))
        def _():
            reply(shift).wait_send()


def body(n, donor_fields, interp_weights, donor_owner, donor_element, geometry, wall_flag, forcing):
    points, derivative, quad = gll_tables()
    stiff = (derivative.T * quad) @ derivative / quad[:, None]
    fields = donor_fields.shape[0]
    elems = geometry.shape[1]
    receptors = donor_element.shape[0]
    slots = 2 * REACH + 1
    nodes = jnp.asarray(points, jnp.float32)
    position = jnp.sum(interp_weights * nodes[None, :, None], axis=1)
    code = (donor_owner[:, 0] * elems + donor_element).astype(jnp.float32)
    request = jnp.concatenate([position, code[None, :]], 0)
    walls = jnp.tile(wall_flag.astype(jnp.float32), (1, elems // wall_flag.shape[1]))
    along_y = np.zeros((8, 8, 8, elems), np.float32) + stiff.T[:, :, None, None]
    along_x = np.zeros((8, 8, elems), np.float32)
    for step in range(8):
        for i in range(8):
            along_x[step, i] = stiff[i, (i - step) % 8]
    plane = np.zeros((8, 8, elems), np.float32) + (quad[:, None] * quad[None, :])[:, :, None]
    groups = CHUNK // 64
    count = receptors // CHUNK
    per_side = count // 2
    place = np.zeros((groups * count, elems), np.float32)
    for group in range(groups):
        for chunk in range(count):
            y = groups * (chunk % per_side) + group
            place[group * count + chunk, y * EX + (EX - 1) * (chunk // per_side)] = 1.0
    cube = (8, 8, 8, elems)
    phases = 4 + ITERS
    vmem = pl.BlockSpec(memory_space=pltpu.VMEM)
    velocity, residual, interface = pl.pallas_call(
        functools.partial(kernel, n),
        out_shape=(
            jax.ShapeDtypeStruct(cube, jnp.float32),
            jax.ShapeDtypeStruct(cube, jnp.float32),
            jax.ShapeDtypeStruct((fields, receptors), jnp.float32),
        ),
        in_specs=[vmem] * 9,
        out_specs=(vmem, vmem, vmem),
        scratch_shapes=[
            pltpu.VMEM((fields * 512, 2 * elems), jnp.bfloat16),
            pltpu.VMEM((slots, 4, receptors), jnp.float32),
            pltpu.VMEM((slots, fields, count, CHUNK), jnp.float32),
            pltpu.VMEM((slots, fields, count, CHUNK), jnp.float32),
            pltpu.VMEM((phases, 2, 8, 8, elems), jnp.float32),
            pltpu.VMEM((phases, 2, 8, 8, elems), jnp.float32),
            pltpu.VMEM((ITERS, 2, 128), jnp.float32),
            pltpu.VMEM((ITERS, n, 2, 128), jnp.float32),
        ]
        + [pltpu.VMEM(cube, jnp.float32)] * 8
        + [pltpu.SemaphoreType.DMA((slots,))] * 4
        + [pltpu.SemaphoreType.DMA((phases, 2))] * 2
        + [pltpu.SemaphoreType.DMA((ITERS, n))] * 2,
        compiler_params=pltpu.CompilerParams(
            collective_id=0, has_side_effects=True, vmem_limit_bytes=48 * 1024 * 1024
        ),
    )(
        request,
        donor_fields,
        geometry,
        walls,
        forcing.reshape(cube),
        jnp.asarray(along_y),
        jnp.asarray(along_x),
        jnp.asarray(plane),
        jnp.asarray(place),
    )
    return (velocity.reshape(512, elems), residual.reshape(512, elems), interface)


def solution(mesh):
    in_specs = (
        P(None, None, ("mesh", "dom")),
        P(None, None, ("mesh", "dom")),
        P(("mesh", "dom"), None),
        P(("mesh", "dom")),
        P(None, ("mesh", "dom")),
        P(None, ("mesh", "dom")),
        P(None, ("mesh", "dom")),
    )
    out_specs = (P(None, ("mesh", "dom")), P(None, ("mesh", "dom")), P(None, ("mesh", "dom")))
    return jax.shard_map(
        functools.partial(body, mesh.shape["dom"]),
        mesh=mesh,
        in_specs=in_specs,
        out_specs=out_specs,
        check_vma=False,
    )
```

time: 587 us -> 70 us (0.12); the launches traced: 576 us -> 69.5 us
  local copies, waits for them, and re-layouts: 193 us -> 8.25 us
  other arithmetic: 150 us -> 3.17 us
  blocking collectives: 122 us -> 0 us
  Pallas kernels: 0 us -> 57.4 us
  starting transfers between devices: 48.8 us -> 0 us
  waiting for transfers between devices: 40.6 us -> 0 us
  between operations: 12.5 us -> 0.67 us
  matrix products: 10.3 us -> 0 us
    psum x3 -> x0, blocking collectives: 122 us -> none  [paired_dots(): lax.psum((jnp.sum(residual_now * precond / multiplicity), jnp.sum(precond...]
    gather x8 -> x0, local copies, waits for them, and re-layouts: 94.6 us -> none  [the longest x5 68.5 us: body(): jnp.take(donor_fields, lookups, axis=2).reshape(field_count, 64, 8, count)]
    select_n x24 -> x0, other arithmetic: 80.7 us -> none  [the longest x5 61.6 us: body(): jnp.take(donor_fields, lookups, axis=2).reshape(field_count, 64, 8, count)]
    select_n x6 -> x0, local copies, waits for them, and re-layouts: 74.5 us -> none  [the longest x5 73.5 us: body(): jnp.take(donor_fields, lookups, axis=2).reshape(field_count, 64, 8, count)]
    pallas_call x0 -> x1, Pallas kernels: none -> 57.4 us  [body(): pl.pallas_call(functools.partial(kernel, n), out_shape=(jax.ShapeDtypeStr...]
    ppermute x20 -> x0, starting transfers between devices: 48.8 us -> none  [the longest x8 24.5 us: from_behind(): lax.ppermute(value, axis, [(source, source + steps) for source in range(l...]
    reduce_sum x19 -> x1, other arithmetic: 46.7 us -> 1.06 us  [body(): position = jnp.sum(interp_weights * nodes[None, :, None], axis=1)]
    ppermute x20 -> x0, waiting for transfers between devices: 40.6 us -> none  [the longest x5 25 us: with_halo(): after = lax.ppermute(leading, axis, down)]
  transfers between devices with their start and end apart: 20 -> 0, of which waited for: 13 -> 0; matrix products, arithmetic and copies ran while one was open for 38% -> 0% of each run, Pallas kernels for 0% -> 0%
where the time goes in v1:
time: 70 us; the launch traced here: 69.5 us
  Pallas kernels  57.4 us (82%)
  local copies, waits for them, and re-layouts  8.25 us (12%)
  other arithmetic  3.17 us (5%)
    pallas_call x1, Pallas kernels, body(): pl.pallas_call(functools.partial(kernel, n), out_shape=(jax.ShapeDtypeStr...  57.4 us
    unnamed x17, local copies, waits for them, and re-layouts  8.16 us

profile of v1, /device:TPU:0, one launch (start us, length us, event | category | flops | bytes accessed | tf_op | source)
XLA Modules:
  0.0 69.5 jit_solution(9792330344700426575)
XLA Ops:
  0.6 0.7 convert_element_type.7
  1.3 0.7 %broadcast_multiply_fusion = s32[2048,1]{0,1:T(1,128)S(1)} fusion(s32[2048,1]{0,1:T(1,128)} %param.14), kind=kLoop, calls=%fused_computation.3 | loop fusion | flops 2048 | bytes 16384 | tf_op jit(solution)/shard_map/mul | solution.py:472
  2.0 0.7 %add_convert_fusion = f32[2048]{0:T(1024)S(1)} fusion(s32[2048]{0:T(1024)S(1)} %bitcast.9, s32[2048]{0:T(1024)} %param.15), kind=kLoop, calls=%fused_computation.2 | loop fusion | flops 4096 | bytes 24576 | tf_op jit(solution)/shard_map/convert_element_type | solution.py:472
  2.7 0.1 tile.10.wall_ref
  2.8 1.1 %multiply_reduce_fusion = f32[3,2048]{1,0:T(4,128)S(1)} fusion(f32[3,8,2048]{2,1,0:T(8,128)} %param.13, f32[8]{0:T(128)} %constant.14.clone), kind=kLoop, calls=%fused_computation | loop fusion | flops 92160 | bytes 221216 | tf_op jit(solution)/shard_map/reduce_sum | solution.py:471
  3.9 0.0 copy-start
  3.9 1.3 %copy-done = f32[5,512,128]{2,1,0:T(8,128)S(1)} copy-done((f32[5,512,128]{2,1,0:T(8,128)S(1)}, f32[5,512,128]{2,1,0:T(8,128)}, u32[]{:S(2)}) %copy-start) | copy-done | bytes 1310744
  5.2 0.0 copy-start.1
  5.2 0.9 %copy-done.1 = f32[512,128]{1,0:T(8,128)S(1)} copy-done((f32[512,128]{1,0:T(8,128)S(1)}, f32[512,128]{1,0:T(8,128)}, u32[]{:S(2)}) %copy-start.1) | copy-done | bytes 262168
  6.2 0.0 copy-start.2
  6.2 0.9 %copy-done.2 = f32[8,8,8,128]{3,2,1,0:T(8,128)S(1)} copy-done((f32[8,8,8,128]{3,2,1,0:T(8,128)S(1)}, f32[8,8,8,128]{3,2,1,0:T(8,128)}, u32[]{:S(2)}) %copy-start.2) | copy-done | bytes 262168
  7.1 0.0 copy-start.3
  7.1 0.8 %copy-done.3 = f32[8,8,128]{2,1,0:T(8,128)S(1)} copy-done((f32[8,8,128]{2,1,0:T(8,128)S(1)}, f32[8,8,128]{2,1,0:T(8,128)}, u32[]{:S(2)}) %copy-start.3) | copy-done | bytes 32792
  7.9 0.0 copy-start.4
  7.9 0.8 %copy-done.4 = f32[8,8,128]{2,1,0:T(8,128)S(1)} copy-done((f32[8,8,128]{2,1,0:T(8,128)S(1)}, f32[8,8,128]{2,1,0:T(8,128)}, u32[]{:S(2)}) %copy-start.4) | copy-done | bytes 32792
  8.6 0.0 copy-start.5
  8.6 0.7 %copy-done.5 = f32[32,128]{1,0:T(8,128)S(1)} copy-done((f32[32,128]{1,0:T(8,128)S(1)}, f32[32,128]{1,0:T(8,128)}, u32[]{:S(2)}) %copy-start.5) | copy-done | bytes 16408
  9.4 0.0 copy-start.6
  9.4 0.7 copy-done.6
  10.0 57.4 %shard_map.139 = (f32[8,8,8,128]{3,2,1,0:T(8,128)S(1)}, f32[8,8,8,128]{3,2,1,0:T(8,128)S(1)}, f32[5,2048]{1,0:T(8,128)S(1)}) custom-call(f32[4,2048]{1,0:T(4,128)S(1)} %pad_maximum_fusion.request_ref, f32[5,512,128]{2,1,0:T(8,128)S(1)} %copy-done, f32[4,128]{1,0:T(4,128)S(1)} %copy-done.6, f32[2,128]{1,0:T(2,128)S(1)} %tile.10.wall_ref, ...), custom_call_target="tpu_custom_call" | custom-call | tf_op jit(solution)/shard_map/pallas_call | solution.py:492
  67.5 0.7 %copy.18 = f32[512,128]{1,0:T(8,128)} copy(f32[512,128]{1,0:T(8,128)S(1)} %bitcast.7) | data formatting | bytes 524288
  68.2 0.7 %copy.19 = f32[512,128]{1,0:T(8,128)} copy(f32[512,128]{1,0:T(8,128)S(1)} %bitcast.6) | data formatting | bytes 524288
  68.9 0.6 copy.20
  (2 shorter events, 0.0 us)
Async XLA Ops:
  3.9 1.3 %copy-start = (f32[5,512,128]{2,1,0:T(8,128)S(1)}, f32[5,512,128]{2,1,0:T(8,128)}, u32[]{:S(2)}) copy-start(f32[5,512,128]{2,1,0:T(8,128)} %donor_ref.1) | copy-start | bytes 3932164
  5.2 0.9 %copy-start.1 = (f32[512,128]{1,0:T(8,128)S(1)}, f32[512,128]{1,0:T(8,128)}, u32[]{:S(2)}) copy-start(f32[512,128]{1,0:T(8,128)} %param.18) | copy-start | bytes 786436
  6.2 0.9 %copy-start.2 = (f32[8,8,8,128]{3,2,1,0:T(8,128)S(1)}, f32[8,8,8,128]{3,2,1,0:T(8,128)}, u32[]{:S(2)}) copy-start(f32[8,8,8,128]{3,2,1,0:T(8,128)} %constant.15.clone.along_y_ref) | copy-start | bytes 786436
  7.1 0.8 %copy-start.3 = (f32[8,8,128]{2,1,0:T(8,128)S(1)}, f32[8,8,128]{2,1,0:T(8,128)}, u32[]{:S(2)}) copy-start(f32[8,8,128]{2,1,0:T(8,128)} %constant.17.clone.plane_ref) | copy-start | bytes 98308
  7.9 0.8 %copy-start.4 = (f32[8,8,128]{2,1,0:T(8,128)S(1)}, f32[8,8,128]{2,1,0:T(8,128)}, u32[]{:S(2)}) copy-start(f32[8,8,128]{2,1,0:T(8,128)} %constant.16.clone.along_x_ref) | copy-start | bytes 98308
  8.6 0.7 %copy-start.5 = (f32[32,128]{1,0:T(8,128)S(1)}, f32[32,128]{1,0:T(8,128)}, u32[]{:S(2)}) copy-start(f32[32,128]{1,0:T(8,128)} %constant.18.clone.place_ref) | copy-start | bytes 49156
  9.4 0.7 copy-start.6

commit v2 on v1

--- a/solution.py
+++ b/solution.py
@@ -49,17 +49,19 @@
 def kernel(
     n,
     request_ref,
-    donor_ref,
+    donor_hbm,
     geometry_ref,
     wall_ref,
+    forcing_hbm,
+    velocity_ref,
+    residual_ref,
+    interface_ref,
+    donor_ref,
     forcing_ref,
     along_y_ref,
     along_x_ref,
     plane_ref,
-    place_ref,
-    velocity_ref,
-    residual_ref,
-    interface_ref,
+    load_sem,
     split,
     asked,
     answer,
@@ -95,6 +97,11 @@
     slab = lax.axis_index("dom")
     other = 1 - mesh_id
 
+    donor_load = pltpu.make_async_copy(donor_hbm, donor_ref, load_sem.at[0])
+    forcing_load = pltpu.make_async_copy(forcing_hbm, forcing_ref, load_sem.at[1])
+    donor_load.start()
+    forcing_load.start()
+
     def inside(index):
         return jnp.logical_and(index >= 0, index < n)
 
@@ -206,6 +213,19 @@
     element = lax.broadcasted_iota(jnp.int32, (8, elems), 1)
     x_index = element % EX
     y_index = element // EX % EY
+
+    across = jnp.zeros((8, elems), jnp.float32)
+    for a in range(8):
+        across = jnp.where(node == a, float(quad[a]), across)
+    for j in range(8):
+        plane_ref[j] = across * float(quad[j])
+        for m in range(8):
+            along_y_ref[m, j] = jnp.full((8, elems), float(stiff[j, m]), jnp.float32)
+    for step in range(8):
+        turned = jnp.zeros((8, elems), jnp.float32)
+        for i in range(8):
+            turned = jnp.where(node == i, float(stiff[i, (i - step) % 8]), turned)
+        along_x_ref[step] = turned
 
     def flag(condition):
         return jnp.where(condition, 1.0, 0.0)
@@ -248,6 +268,7 @@
     send_faces(0)
     send_faces(1)
 
+    donor_load.wait()
     donors = donor_ref[...].reshape(fields * 512, elems)
     coarse = donors.astype(jnp.bfloat16)
     split[:, :elems] = coarse
@@ -352,9 +373,15 @@
     rows = interface_sum[0]
     groups = CHUNK // 64
     rows = jnp.concatenate([rows[:, t * 64 : (t + 1) * 64] for t in range(groups)], 0)
+    count = receptors // CHUNK
+    per_side = count // 2
+    row = lax.broadcasted_iota(jnp.int32, (groups * count, elems), 0)
+    spot = lax.broadcasted_iota(jnp.int32, (groups * count, elems), 1)
+    piece = row % count
+    target = (groups * (piece % per_side) + row // count) * EX + (EX - 1) * (piece // per_side)
     placed = lax.dot_general(
         rows,
-        place_ref[...],
+        flag(spot == target),
         (((0,), (0,)), ((), ())),
         precision=lax.Precision.HIGHEST,
         preferred_element_type=jnp.float32,
@@ -389,6 +416,7 @@
         total = g_x * along_x + g_y * along_y + g_z * along_z + g_m * tile
         return weights(layer) * total
 
+    forcing_load.wait()
     for layer in ORDER:
         loaded = weights(layer) * g_m * forcing_ref[layer] - local_tile(boundary, layer)
         residual_ref[layer] = plane_sum(loaded)
@@ -461,8 +489,7 @@
 
 
 def body(n, donor_fields, interp_weights, donor_owner, donor_element, geometry, wall_flag, forcing):
-    points, derivative, quad = gll_tables()
-    stiff = (derivative.T * quad) @ derivative / quad[:, None]
+    points, _, _ = gll_tables()
     fields = donor_fields.shape[0]
     elems = geometry.shape[1]
     receptors = donor_element.shape[0]
@@ -472,23 +499,11 @@
     code = (donor_owner[:, 0] * elems + donor_element).astype(jnp.float32)
     request = jnp.concatenate([position, code[None, :]], 0)
     walls = jnp.tile(wall_flag.astype(jnp.float32), (1, elems // wall_flag.shape[1]))
-    along_y = np.zeros((8, 8, 8, elems), np.float32) + stiff.T[:, :, None, None]
-    along_x = np.zeros((8, 8, elems), np.float32)
-    for step in range(8):
-        for i in range(8):
-            along_x[step, i] = stiff[i, (i - step) % 8]
-    plane = np.zeros((8, 8, elems), np.float32) + (quad[:, None] * quad[None, :])[:, :, None]
-    groups = CHUNK // 64
     count = receptors // CHUNK
-    per_side = count // 2
-    place = np.zeros((groups * count, elems), np.float32)
-    for group in range(groups):
-        for chunk in range(count):
-            y = groups * (chunk % per_side) + group
-            place[group * count + chunk, y * EX + (EX - 1) * (chunk // per_side)] = 1.0
     cube = (8, 8, 8, elems)
     phases = 4 + ITERS
     vmem = pl.BlockSpec(memory_space=pltpu.VMEM)
+    hbm = pl.BlockSpec(memory_space=pl.ANY)
     velocity, residual, interface = pl.pallas_call(
         functools.partial(kernel, n),
         out_shape=(
@@ -496,9 +511,15 @@
             jax.ShapeDtypeStruct(cube, jnp.float32),
             jax.ShapeDtypeStruct((fields, receptors), jnp.float32),
         ),
-        in_specs=[vmem] * 9,
+        in_specs=[vmem, hbm, vmem, vmem, hbm],
         out_specs=(vmem, vmem, vmem),
         scratch_shapes=[
+            pltpu.VMEM((fields, 512, elems), jnp.float32),
+            pltpu.VMEM(cube, jnp.float32),
+            pltpu.VMEM(cube, jnp.float32),
+            pltpu.VMEM((8, 8, elems), jnp.float32),
+            pltpu.VMEM((8, 8, elems), jnp.float32),
+            pltpu.SemaphoreType.DMA((2,)),
             pltpu.VMEM((fields * 512, 2 * elems), jnp.bfloat16),
             pltpu.VMEM((slots, 4, receptors), jnp.float32),
             pltpu.VMEM((slots, fields, count, CHUNK), jnp.float32),
@@ -521,10 +542,6 @@
         geometry,
         walls,
         forcing.reshape(cube),
-        jnp.asarray(along_y),
-        jnp.asarray(along_x),
-        jnp.asarray(plane),
-        jnp.asarray(place),
     )
     return (velocity.reshape(512, elems), residual.reshape(512, elems), interface)
 

time: 70 us -> 66.7 us (0.953)
  local copies, waits for them, and re-layouts: 8.25 us -> 5.07 us
    unnamed x17 -> x9, local copies, waits for them, and re-layouts: 8.16 us -> 4.98 us
where the time goes in v2:
time: 66.7 us; the launch traced here: 66.4 us
  Pallas kernels  57.5 us (86%)
  local copies, waits for them, and re-layouts  5.07 us (8%)
  other arithmetic  3.17 us (5%)
    pallas_call x1, Pallas kernels, body(): pl.pallas_call(functools.partial(kernel, n), out_shape=(jax.ShapeDtypeStr...  57.5 us
    unnamed x9, local copies, waits for them, and re-layouts  4.98 us

profile of v2, /device:TPU:0, one launch (start us, length us, event | category | flops | bytes accessed | tf_op | source)
XLA Modules:
  0.0 66.4 jit_solution(8760335562207359234)
XLA Ops:
  0.6 0.7 %convert_element_type.7 = f32[2,8]{1,0:T(2,128)S(1)} convert(s32[2,8]{1,0:T(2,128)} %param.13) | non-fusion elementwise | flops 16 | bytes 128 | tf_op jit(solution)/shard_map/convert_element_type | solution.py:501
  1.3 0.7 %broadcast_multiply_fusion = s32[2048,1]{0,1:T(1,128)S(1)} fusion(s32[2048,1]{0,1:T(1,128)} %param.10), kind=kLoop, calls=%fused_computation.3 | loop fusion | flops 2048 | bytes 16384 | tf_op jit(solution)/shard_map/mul | solution.py:499
  2.0 0.7 %add_convert_fusion = f32[2048]{0:T(1024)S(1)} fusion(s32[2048]{0:T(1024)S(1)} %bitcast.9, s32[2048]{0:T(1024)} %param.11), kind=kLoop, calls=%fused_computation.2 | loop fusion | flops 4096 | bytes 24576 | tf_op jit(solution)/shard_map/convert_element_type | solution.py:499
  2.7 0.1 tile.10.wall_ref
  2.8 1.1 %multiply_reduce_fusion = f32[3,2048]{1,0:T(4,128)S(1)} fusion(f32[3,8,2048]{2,1,0:T(8,128)} %param.9, f32[8]{0:T(128)} %constant.6.clone), kind=kLoop, calls=%fused_computation | loop fusion | flops 92160 | bytes 221216 | tf_op jit(solution)/shard_map/reduce_sum | solution.py:498
  3.9 0.0 copy-start
  3.9 1.3 %copy-done = f32[5,512,128]{2,1,0:T(8,128)S(1)} copy-done((f32[5,512,128]{2,1,0:T(8,128)S(1)}, f32[5,512,128]{2,1,0:T(8,128)}, u32[]{:S(2)}) %copy-start) | copy-done | bytes 1310744
  5.2 0.0 copy-start.1
  5.2 0.9 %copy-done.1 = f32[512,128]{1,0:T(8,128)S(1)} copy-done((f32[512,128]{1,0:T(8,128)S(1)}, f32[512,128]{1,0:T(8,128)}, u32[]{:S(2)}) %copy-start.1) | copy-done | bytes 262168
  6.2 0.0 copy-start.2
  6.2 0.7 %copy-done.2 = f32[4,128]{1,0:T(4,128)S(1)} copy-done((f32[4,128]{1,0:T(4,128)S(1)}, f32[4,128]{1,0:T(4,128)}, u32[]{:S(2)}) %copy-start.2) | copy-done | bytes 2072
  6.9 57.5 %shard_map.103 = (f32[8,8,8,128]{3,2,1,0:T(8,128)S(1)}, f32[8,8,8,128]{3,2,1,0:T(8,128)S(1)}, f32[5,2048]{1,0:T(8,128)S(1)}) custom-call(f32[4,2048]{1,0:T(4,128)S(1)} %pad_maximum_fusion.request_ref, f32[5,512,128]{2,1,0:T(8,128)S(1)} %copy-done, f32[4,128]{1,0:T(4,128)S(1)} %copy-done.2, f32[2,128]{1,0:T(2,128)S(1)} %tile.10.wall_ref, ...), custom_call_target="tpu_custom_call" | custom-call | tf_op jit(solution)/shard_map/pallas_call | solution.py:507
  64.4 0.7 %copy.14 = f32[512,128]{1,0:T(8,128)} copy(f32[512,128]{1,0:T(8,128)S(1)} %bitcast.6) | data formatting | bytes 524288
  65.1 0.7 %copy.15 = f32[512,128]{1,0:T(8,128)} copy(f32[512,128]{1,0:T(8,128)S(1)} %bitcast.5) | data formatting | bytes 524288
  65.8 0.6 copy.16
  (2 shorter events, 0.0 us)
Async XLA Ops:
  3.9 1.3 %copy-start = (f32[5,512,128]{2,1,0:T(8,128)S(1)}, f32[5,512,128]{2,1,0:T(8,128)}, u32[]{:S(2)}) copy-start(f32[5,512,128]{2,1,0:T(8,128)} %donor_hbm.1) | copy-start | bytes 3932164
  5.2 0.9 %copy-start.1 = (f32[512,128]{1,0:T(8,128)S(1)}, f32[512,128]{1,0:T(8,128)}, u32[]{:S(2)}) copy-start(f32[512,128]{1,0:T(8,128)} %param.14) | copy-start | bytes 786436
  6.2 0.7 %copy-start.2 = (f32[4,128]{1,0:T(4,128)S(1)}, f32[4,128]{1,0:T(4,128)}, u32[]{:S(2)}) copy-start(f32[4,128]{1,0:T(4,128)} %geometry_ref.1) | copy-start | bytes 6148
